TPU v7x, 32 devices: a whole 2x2x4 slice. The times are simulated.
32 devices in a mesh: ctx: 8 (over z, x), heads: 4 (over y, core).
Axes of the slice: x: 2, y: 2, z: 4, core: 2. Of those that a mesh axis runs over, the one named last changes fastest.
Arguments:
- activations: bfloat16 [2048, 8192], P('ctx', 'heads'), may hold values from -20 to 20
- w_query: bfloat16 [8192, 4096], P(None, 'heads'), may hold values from -0.0625 to 0.0625
- w_key: bfloat16 [8192, 1024], P(None, 'heads'), may hold values from -0.0625 to 0.0625
- w_value: bfloat16 [8192, 1024], P(None, 'heads'), may hold values from -0.0625 to 0.0625
- doc_lengths: int32 [8], replicated, may hold values from 1 to 1024, 2048 in all
- block_dest: int32 [32], replicated, may hold values from 0 to 7, as said below
- out_grad: bfloat16 [2048, 4096], P('ctx', 'heads'), may hold values from -6 to 6
Outputs:
- attention: bfloat16 [2048, 4096], P('ctx', 'heads')
- input_grad: bfloat16 [2048, 8192], P('ctx', 'heads')
Inputs may be any that keep to these rules, and one draw needn't show every extreme that they name: `block_dest`: loader block b lies on loader shard b // 4. Each loader shard sends its blocks to different context shards, and each context shard receives exactly 4 blocks, from different loader shards.
All inputs are finite; a program needn't handle non-finite values.
Results may differ from a plain program's by a relative error of at most 0.025.
The roundings to bfloat16 on the way count: a program that leaves them out, or rounds other values in their place, can miss the bound.
Values may be sent and summed in bfloat16 or wider, within the bound.
A program may use at most 128 MiB of HBM per device.

v0:
```python
import math
import jax
import jax.numpy as jnp
from jax import lax
from jax.sharding import PartitionSpec as P

HD = 128
QPK = 4
NEG = -1e30


def from_behind(value, axis, steps):
    count = lax.axis_size(axis)
    pairs = [(source, (source + steps) % count) for source in range(count)]
    return lax.ppermute(value, axis, pairs)


def layout(block_dest, block_rows):
    nblk = block_dest.shape[0]
    index = jnp.arange(nblk, dtype=jnp.int32)
    order_key = block_dest * nblk + index
    ranks = jnp.sum((order_key[None, :] < order_key[:, None]).astype(jnp.int32), axis=1)
    ctx_blocks = jnp.sum(jnp.where(ranks[None, :] == index[:, None], index[None, :], 0), axis=1)
    ctx_pos = (
        ctx_blocks[:, None] * block_rows + jnp.arange(block_rows, dtype=jnp.int32)[None, :]
    ).reshape(-1)
    return (ctx_blocks, ctx_pos)


def doc_ids(positions, doc_lengths):
    ends = jnp.cumsum(doc_lengths)
    return jnp.sum((ends[None, :] <= positions[:, None]).astype(jnp.int32), axis=1)


def spread(table, array, block_rows):
    width = array.shape[-1]
    grouped = array.reshape(table.shape[1], block_rows, width)
    moved = jnp.einsum("ab,brf->arf", table, grouped, preferred_element_type=jnp.float32)
    return moved.astype(jnp.bfloat16)


def transposed_dot(left, weight):
    return lax.dot_general(
        left, weight, (((1,), (1,)), ((), ())), preferred_element_type=jnp.float32
    )


def per_device(activations, w_query, w_key, w_value, doc_lengths, block_dest, out_grad):
    ctx_count = lax.axis_size("ctx")
    ctx_rank = lax.axis_index("ctx")
    tok_dev = activations.shape[0]
    block_rows = tok_dev * ctx_count // block_dest.shape[0]
    blocks_here = tok_dev // block_rows
    head_dim = HD
    groups = w_key.shape[1] // head_dim
    per_group = QPK
    scale = 1.0 / math.sqrt(head_dim)
    ctx_blocks, ctx_pos = layout(block_dest, block_rows)
    ctx_doc = doc_ids(ctx_pos, doc_lengths)
    my_pos = lax.dynamic_slice_in_dim(ctx_pos, ctx_rank * tok_dev, tok_dev, 0)
    my_doc = lax.dynamic_slice_in_dim(ctx_doc, ctx_rank * tok_dev, tok_dev, 0)
    piece = lax.all_gather(activations, "heads", axis=1, tiled=True)
    rows = piece.shape[1]
    proj_q = jnp.dot(piece, w_query, preferred_element_type=jnp.float32)
    proj_k = jnp.dot(piece, w_key, preferred_element_type=jnp.float32)
    proj_v = jnp.dot(piece, w_value, preferred_element_type=jnp.float32)
    loader_q = proj_q.astype(jnp.bfloat16)
    loader_k = proj_k.astype(jnp.bfloat16)
    loader_v = proj_v.astype(jnp.bfloat16)
    slots = jnp.arange(ctx_count, dtype=jnp.int32)
    my_dest = lax.dynamic_slice_in_dim(block_dest, ctx_rank * blocks_here, blocks_here, 0)
    send_map = (my_dest[None, :] == slots[:, None]).astype(jnp.bfloat16)
    mine = lax.dynamic_slice_in_dim(ctx_blocks, ctx_rank * blocks_here, blocks_here, 0)
    source = mine // blocks_here
    take_map = (source[:, None] == slots[None, :]).astype(jnp.bfloat16)
    recv_q, recv_k, recv_v = (
        lax.all_to_all(
            spread(send_map, loader_q, block_rows), "ctx", split_axis=0, concat_axis=0, tiled=True
        ),
        lax.all_to_all(
            spread(send_map, loader_k, block_rows), "ctx", split_axis=0, concat_axis=0, tiled=True
        ),
        lax.all_to_all(
            spread(send_map, loader_v, block_rows), "ctx", split_axis=0, concat_axis=0, tiled=True
        ),
    )
    ctx_q = spread(take_map, recv_q.reshape(ctx_count * block_rows, -1), block_rows).reshape(
        tok_dev, -1
    )
    ctx_k = spread(take_map, recv_k.reshape(ctx_count * block_rows, -1), block_rows).reshape(
        tok_dev, -1
    )
    ctx_v = spread(take_map, recv_v.reshape(ctx_count * block_rows, -1), block_rows).reshape(
        tok_dev, -1
    )
    query_four = ctx_q.reshape(tok_dev, groups, per_group, head_dim)

    def visible(key_pos, key_doc):
        return (my_doc[:, None] == key_doc[None, :]) & (key_pos[None, :] <= my_pos[:, None])

    def attend(state, key_blk, value_blk, key_pos, key_doc):
        mask = visible(key_pos, key_doc)

        def attend_run(inner):
            m_old, l_old, accum = inner
            scores = (
                jnp.einsum(
                    "tgqe,sge->gqts", query_four, key_blk, preferred_element_type=jnp.float32
                )
                * scale
            )
            scores = jnp.where(mask[None, None], scores, NEG)
            m_new = jnp.maximum(m_old, jnp.max(scores, axis=-1))
            factor = jnp.exp(m_old - m_new)
            probs = jnp.where(mask[None, None], jnp.exp(scores - m_new[..., None]), 0.0)
            l_new = l_old * factor + jnp.sum(probs, axis=-1)
            accum = accum * factor[..., None] + jnp.einsum(
                "gqts,sge->gqte",
                probs,
                value_blk.astype(jnp.float32),
                precision=lax.Precision.HIGHEST,
                preferred_element_type=jnp.float32,
            )
            return (m_new, l_new, accum)

        return lax.cond(jnp.any(mask), attend_run, lambda inner: inner, state)

    start_state = (
        jnp.full((groups, per_group, tok_dev), NEG, jnp.float32),
        jnp.zeros((groups, per_group, tok_dev), jnp.float32),
        jnp.zeros((groups, per_group, tok_dev, head_dim), jnp.float32),
    )
    grad_four = out_grad.reshape(tok_dev, groups, per_group, head_dim)

    def grads_over(dquery, key_piece, value_piece, start, lse, delta):
        rows = key_piece.shape[0]
        width = math.gcd(rows, 512)

        def grads_one_block(index, inner):
            dq_sum, dk_rows, dv_rows = inner
            offset = index * width
            key_blk = key_piece.reshape(width, groups, head_dim)
            value_blk = value_piece.reshape(width, groups, head_dim)
            key_pos = lax.dynamic_slice_in_dim(ctx_pos, start + offset, width, 0)
            key_doc = lax.dynamic_slice_in_dim(ctx_doc, start + offset, width, 0)
            mask = visible(key_pos, key_doc)

            def one_run(unused):
                scores = (
                    jnp.einsum(
                        "tgqe,sge->gqts", query_four, key_blk, preferred_element_type=jnp.float32
                    )
                    * scale
                )
                weights = jnp.where(mask[None, None], jnp.exp(scores - lse[..., None]), 0.0)
                weights_b = weights.astype(jnp.bfloat16)
                dv_blk = jnp.einsum(
                    "gqts,tgqe->sge", weights_b, grad_four, preferred_element_type=jnp.float32
                )
                dprob = jnp.einsum(
                    "tgqe,sge->gqts", grad_four, value_blk, preferred_element_type=jnp.float32
                )
                dscore = (weights * (dprob - delta[..., None]) * scale).astype(jnp.bfloat16)
                dq_add = jnp.einsum(
                    "gqts,sge->tgqe", dscore, key_blk, preferred_element_type=jnp.float32
                )
                dk_blk = jnp.einsum(
                    "gqts,tgqe->sge", dscore, query_four, preferred_element_type=jnp.float32
                )
                return (dq_add, dk_blk, dv_blk)

            def skip(unused):
                return (
                    jnp.zeros((tok_dev, groups, per_group, head_dim), jnp.float32),
                    jnp.zeros((width, groups, head_dim), jnp.float32),
                    jnp.zeros((width, groups, head_dim), jnp.float32),
                )

            dq_add, dk_blk, dv_blk = lax.cond(jnp.any(mask), one_run, skip, 0)
            dk_rows = dk_blk.reshape(width, groups * head_dim)
            dv_rows = dv_blk.reshape(width, groups * head_dim)
            return (dq_sum + dq_add, dk_rows, dv_rows)

        empty_rows = jnp.zeros((rows, groups * head_dim), jnp.float32)
        return lax.fori_loop(0, rows // width, grads_one_block, (dquery, empty_rows, empty_rows))

    dq_start = jnp.zeros((tok_dev, groups, per_group, head_dim), jnp.float32)
    key_piece = lax.all_gather(ctx_k, "ctx", axis=0, tiled=True)
    value_piece = lax.all_gather(ctx_v, "ctx", axis=0, tiled=True)
    rows = key_piece.shape[0]
    width = math.gcd(rows, 512)

    def fold_one_block(index, inner):
        offset = index * width
        key_blk = lax.dynamic_slice_in_dim(key_piece, offset, width, 0).reshape(
            width, groups, head_dim
        )
        value_blk = lax.dynamic_slice_in_dim(value_piece, offset, width, 0).reshape(
            width, groups, head_dim
        )
        key_pos = lax.dynamic_slice_in_dim(ctx_pos, offset, width, 0)
        key_doc = lax.dynamic_slice_in_dim(ctx_doc, offset, width, 0)
        return attend(inner, key_blk, value_blk, key_pos, key_doc)

    m_end, l_end, accum = lax.fori_loop(0, rows // width, fold_one_block, start_state)
    attn = (accum / l_end[..., None]).astype(jnp.bfloat16)
    attention = attn.transpose(2, 0, 1, 3).reshape(tok_dev, groups * per_group * head_dim)
    lse = m_end + jnp.log(l_end)
    attn_four = attention.reshape(tok_dev, groups, per_group, head_dim)
    delta = jnp.einsum(
        "tgqe,tgqe->gqt", grad_four.astype(jnp.float32), attn_four.astype(jnp.float32)
    )

    def turn(step, inner):
        dquery, key_now, value_now, dk_now, dv_now = inner
        owner = jnp.mod(ctx_rank - step, ctx_count)
        dquery, dk_add, dv_add = grads_over(dquery, key_now, value_now, owner * tok_dev, lse, delta)
        dk_now, dv_now = (
            from_behind((dk_now + dk_add).astype(jnp.bfloat16), "ctx", 1).astype(jnp.float32),
            from_behind((dv_now + dv_add).astype(jnp.bfloat16), "ctx", 1).astype(jnp.float32),
        )
        key_now, value_now = from_behind((key_now, value_now), "ctx", 1)
        return (dquery, key_now, value_now, dk_now, dv_now)

    zero_grads = jnp.zeros((tok_dev, groups * head_dim), jnp.float32)
    dquery, unused_k, unused_v, dkey, dvalue = lax.fori_loop(
        0, ctx_count, turn, (dq_start, ctx_k, ctx_v, zero_grads, zero_grads)
    )
    dq_ctx = dquery.reshape(tok_dev, groups * per_group * head_dim).astype(jnp.bfloat16)
    dk_ctx = dkey.astype(jnp.bfloat16)
    dv_ctx = dvalue.astype(jnp.bfloat16)
    back_map = take_map.T
    home_q, home_k, home_v = (
        lax.all_to_all(
            spread(back_map, dq_ctx, block_rows), "ctx", split_axis=0, concat_axis=0, tiled=True
        ),
        lax.all_to_all(
            spread(back_map, dk_ctx, block_rows), "ctx", split_axis=0, concat_axis=0, tiled=True
        ),
        lax.all_to_all(
            spread(back_map, dv_ctx, block_rows), "ctx", split_axis=0, concat_axis=0, tiled=True
        ),
    )
    pick_map = send_map.T
    dq_loader = spread(pick_map, home_q.reshape(ctx_count * block_rows, -1), block_rows).reshape(
        tok_dev, -1
    )
    dk_loader = spread(pick_map, home_k.reshape(ctx_count * block_rows, -1), block_rows).reshape(
        tok_dev, -1
    )
    dv_loader = spread(pick_map, home_v.reshape(ctx_count * block_rows, -1), block_rows).reshape(
        tok_dev, -1
    )
    grad_terms = (
        transposed_dot(dq_loader, w_query)
        + transposed_dot(dk_loader, w_key)
        + transposed_dot(dv_loader, w_value)
    )
    input_grad = lax.psum_scatter(
        grad_terms.astype(jnp.bfloat16), "heads", scatter_dimension=1, tiled=True
    )
    return (attention, input_grad)


def solution(mesh):
    return jax.shard_map(
        per_device,
        mesh=mesh,
        in_specs=(
            P("ctx", "heads"),
            P(None, "heads"),
            P(None, "heads"),
            P(None, "heads"),
            P(),
            P(),
            P("ctx", "heads"),
        ),
        out_specs=(P("ctx", "heads"), P("ctx", "heads")),
        check_vma=False,
    )
```

profile of v0, /device:TPU:0, one launch (start us, length us, event | category | flops | bytes accessed | tf_op | source)
XLA Modules:
  0.0 553.3 jit_solution(3324979120740839685)
XLA Ops:
  9.7 37.1 %all-gather.4.cloned.1.call-done = bf16[256,8192]{1,0:T(8,128)(2,1)} async-done(((bf16[256,2048]{1,0:T(8,128)(2,1)}), bf16[256,8192]{1,0:T(8,128)(2,1)}) %all-gather.4.cloned.1.call-update) | async-done | bytes 4194320 | tf_op jit(solution)/shard_map/all_gather | solution.py:62
  72.1 11.5 %convolution_convert_fusion.4 = bf16[256,1024]{1,0:T(8,128)(2,1)S(1)} fusion(bf16[256,8192]{1,0:T(8,128)(2,1)} %all-gather.4.cloned.1.call-done, bf16[8192,1024]{1,0:T(8,128)(2,1)} %param.16), kind=kOutput, calls=%fused_computation.45 | convolution fusion | flops 4295229440 | bytes 21495808 | tf_op jit(solution)/shard_map/dot_general | solution.py:64
  85.8 6.0 %all-to-all-start.1 = ((bf16[8,64,1024]{2,1,0:T(8,128)(2,1)}), bf16[8,64,1024]{2,1,0:T(8,128)(2,1)S(1)}, u32[]{:S(2)}, u32[]{:S(2)}) async-start(bf16[8,64,1024]{2,1,0:T(8,128)(2,1)} %copy.107), calls=%async_computation.1 | async-start | bytes 2097152 | tf_op jit(solution)/shard_map/all_to_all | solution.py:77
  98.1 27.5 %all-to-all-done.1 = bf16[8,64,1024]{2,1,0:T(8,128)(2,1)S(1)} async-done(((bf16[8,64,1024]{2,1,0:T(8,128)(2,1)}), bf16[8,64,1024]{2,1,0:T(8,128)(2,1)S(1)}, u32[]{:S(2)}, u32[]{:S(2)}) %all-to-all-start.1) | async-done | bytes 1048608 | tf_op jit(solution)/shard_map/all_to_all | solution.py:77
  129.8 36.9 %all-gather.6.cloned.1.call-done = bf16[2048,256]{1,0:T(8,128)(2,1)} async-done(((bf16[256,256]{1,0:T(8,128)(2,1)}), bf16[2048,256]{1,0:T(8,128)(2,1)}) %all-gather.6.cloned.1.call-update) | async-done | bytes 1048592 | tf_op jit(solution)/shard_map/all_gather | solution.py:188
  170.0 47.4 %while.56 = (s32[]{:T(128)}, f32[2,4,256]{2,1,0:T(4,128)S(1)}, f32[2,4,256]{2,1,0:T(4,128)S(1)}, f32[2,4,256,128]{3,2,1,0:T(8,128)}, s32[256]{0:T(256)}, /*index...) while((s32[]{:T(128)}, f32[2,4,256]{2,1,0:T(4,128)S(1)}, ...), condition=%wide.region_10.11_spmd, body=%wide.region_4.10_spmd.sunk | while | flops 1892683776 | bytes 25835900 | solution.py:205
  173.7 8.2 %conditional.5 = ((f32[2,4,256]{2,1,0:T(4,128)S(1)}, f32[2,4,256]{2,1,0:T(4,128)S(1)}, f32[2,4,256,128]{3,2,1,0:T(8,128)})) conditional(s32[]{:T(128)} %convert_element_type.201, (f32[2,4,256]{2,1,0:T(4,128)S(1)}, f32[2,4,256]{2,1,0:T(4,128)S(1)}, f32[2,4,256,128]{3,2,1,0:T(8,128)}) %tuple.116, (pred[256,512]{0,1:T(8,128)(4,1)S(1)}, ...), branch_computations={%region_6.6_spmd, %region_7.9_spmd} | conditional | flops 1892159488 | bytes 25690204 | solution.py:126
  185.5 8.2 %conditional.5 = ((f32[2,4,256]{2,1,0:T(4,128)S(1)}, f32[2,4,256]{2,1,0:T(4,128)S(1)}, f32[2,4,256,128]{3,2,1,0:T(8,128)})) conditional(s32[]{:T(128)} %convert_element_type.201, (f32[2,4,256]{2,1,0:T(4,128)S(1)}, f32[2,4,256]{2,1,0:T(4,128)S(1)}, f32[2,4,256,128]{3,2,1,0:T(8,128)}) %tuple.116, (pred[256,512]{0,1:T(8,128)(4,1)S(1)}, ...), branch_computations={%region_6.6_spmd, %region_7.9_spmd} | conditional | flops 1892159488 | bytes 25690204 | solution.py:126
  197.4 8.2 %conditional.5 = ((f32[2,4,256]{2,1,0:T(4,128)S(1)}, f32[2,4,256]{2,1,0:T(4,128)S(1)}, f32[2,4,256,128]{3,2,1,0:T(8,128)})) conditional(s32[]{:T(128)} %convert_element_type.201, (f32[2,4,256]{2,1,0:T(4,128)S(1)}, f32[2,4,256]{2,1,0:T(4,128)S(1)}, f32[2,4,256,128]{3,2,1,0:T(8,128)}) %tuple.116, (pred[256,512]{0,1:T(8,128)(4,1)S(1)}, ...), branch_computations={%region_6.6_spmd, %region_7.9_spmd} | conditional | flops 1892159488 | bytes 25690204 | solution.py:126
  209.2 8.2 %conditional.5 = ((f32[2,4,256]{2,1,0:T(4,128)S(1)}, f32[2,4,256]{2,1,0:T(4,128)S(1)}, f32[2,4,256,128]{3,2,1,0:T(8,128)})) conditional(s32[]{:T(128)} %convert_element_type.201, (f32[2,4,256]{2,1,0:T(4,128)S(1)}, f32[2,4,256]{2,1,0:T(4,128)S(1)}, f32[2,4,256,128]{3,2,1,0:T(8,128)}) %tuple.116, (pred[256,512]{0,1:T(8,128)(4,1)S(1)}, ...), branch_computations={%region_6.6_spmd, %region_7.9_spmd} | conditional | flops 1892159488 | bytes 25690204 | solution.py:126
  222.4 202.9 %while.57 = (s32[]{:T(128)}, f32[256,2,4,128]{3,0,2,1:T(8,128)S(1)}, bf16[256,256]{1,0:T(8,128)(2,1)}, bf16[256,256]{1,0:T(8,128)(2,1)}, f32[256,256]{0,1:T(8,12...) while((s32[]{:T(128)}, ...), condition=%wide.region_15.16_spmd.clone, body=%wide.region_11.15_spmd.clone.sunk | while | flops 676593664 | bytes 24142468 | solution.py:226
  231.7 5.6 %conditional.6 = (f32[256,2,4,128]{3,0,2,1:T(8,128)S(1)}, f32[256,256]{0,1:T(8,128)S(1)}, f32[256,256]{0,1:T(8,128)S(1)}) conditional(s32[]{:T(128)} %convert_element_type.204, () %tuple.120, (pred[256,256]{0,1:T(8,128)(4,1)}, bf16[256,256]{1,0:T(8,128)(2,1)}, bf16[256,2,4,128]{0,3,2,1:T(8,128)(2,1)}, f32[2,4,256]{2,1,0:T(4,128)}, ...), branch_computations={%region_13.13_spmd, %region_14.14_spmd} | conditional | flops 675282944 | bytes 16203828 | solution.py:179
  304.1 5.6 %conditional.6 = (f32[256,2,4,128]{3,0,2,1:T(8,128)S(1)}, f32[256,256]{0,1:T(8,128)S(1)}, f32[256,256]{0,1:T(8,128)S(1)}) conditional(s32[]{:T(128)} %convert_element_type.204, () %tuple.120, (pred[256,256]{0,1:T(8,128)(4,1)}, bf16[256,256]{1,0:T(8,128)(2,1)}, bf16[256,2,4,128]{0,3,2,1:T(8,128)(2,1)}, f32[2,4,256]{2,1,0:T(4,128)}, ...), branch_computations={%region_13.13_spmd, %region_14.14_spmd} | conditional | flops 675282944 | bytes 16203828 | solution.py:179
  331.5 5.6 %conditional.6 = (f32[256,2,4,128]{3,0,2,1:T(8,128)S(1)}, f32[256,256]{0,1:T(8,128)S(1)}, f32[256,256]{0,1:T(8,128)S(1)}) conditional(s32[]{:T(128)} %convert_element_type.204, () %tuple.120, (pred[256,256]{0,1:T(8,128)(4,1)}, bf16[256,256]{1,0:T(8,128)(2,1)}, bf16[256,2,4,128]{0,3,2,1:T(8,128)(2,1)}, f32[2,4,256]{2,1,0:T(4,128)}, ...), branch_computations={%region_13.13_spmd, %region_14.14_spmd} | conditional | flops 675282944 | bytes 16203828 | solution.py:179
  339.2 7.0 %collective-permute-done.3 = bf16[256,256]{0,1:T(8,128)(2,1)S(1)} collective-permute-done((bf16[256,256]{0,1:T(8,128)(2,1)S(1)}, bf16[256,256]{0,1:T(8,128)(2,1)S(1)}, u32[]{:S(2)}, u32[]{:S(2)}) %collective-permute-start.3) | collective-permute-done | bytes 131104 | tf_op jit(solution)/shard_map/while/body/eval_jaxpr/ppermute | solution.py:15
  357.0 5.6 %conditional.6 = (f32[256,2,4,128]{3,0,2,1:T(8,128)S(1)}, f32[256,256]{0,1:T(8,128)S(1)}, f32[256,256]{0,1:T(8,128)S(1)}) conditional(s32[]{:T(128)} %convert_element_type.204, () %tuple.120, (pred[256,256]{0,1:T(8,128)(4,1)}, bf16[256,256]{1,0:T(8,128)(2,1)}, bf16[256,2,4,128]{0,3,2,1:T(8,128)(2,1)}, f32[2,4,256]{2,1,0:T(4,128)}, ...), branch_computations={%region_13.13_spmd, %region_14.14_spmd} | conditional | flops 675282944 | bytes 16203828 | solution.py:179
  408.2 5.6 %conditional.6 = (f32[256,2,4,128]{3,0,2,1:T(8,128)S(1)}, f32[256,256]{0,1:T(8,128)S(1)}, f32[256,256]{0,1:T(8,128)S(1)}) conditional(s32[]{:T(128)} %convert_element_type.204, () %tuple.120, (pred[256,256]{0,1:T(8,128)(4,1)}, bf16[256,256]{1,0:T(8,128)(2,1)}, bf16[256,2,4,128]{0,3,2,1:T(8,128)(2,1)}, f32[2,4,256]{2,1,0:T(4,128)}, ...), branch_computations={%region_13.13_spmd, %region_14.14_spmd} | conditional | flops 675282944 | bytes 16203828 | solution.py:179
  416.9 6.0 %collective-permute-done.3 = bf16[256,256]{0,1:T(8,128)(2,1)S(1)} collective-permute-done((bf16[256,256]{0,1:T(8,128)(2,1)S(1)}, bf16[256,256]{0,1:T(8,128)(2,1)S(1)}, u32[]{:S(2)}, u32[]{:S(2)}) %collective-permute-start.3) | collective-permute-done | bytes 131104 | tf_op jit(solution)/shard_map/while/body/eval_jaxpr/ppermute | solution.py:15
  432.1 6.0 %all-to-all-done.5 = bf16[8,64,256]{2,1,0:T(8,128)(2,1)S(1)} async-done(((bf16[8,64,256]{2,1,0:T(8,128)(2,1)}), bf16[8,64,256]{2,1,0:T(8,128)(2,1)S(1)}, u32[]{:S(2)}, u32[]{:S(2)}) %all-to-all-start.5) | async-done | bytes 262176 | tf_op jit(solution)/shard_map/all_to_all | solution.py:240
  444.8 9.6 %all-to-all-done.4 = bf16[8,64,256]{2,1,0:T(8,128)(2,1)S(1)} async-done(((bf16[8,64,256]{2,1,0:T(8,128)(2,1)}), bf16[8,64,256]{2,1,0:T(8,128)(2,1)S(1)}, u32[]{:S(2)}, u32[]{:S(2)}) %all-to-all-start.4) | async-done | bytes 262176 | tf_op jit(solution)/shard_map/all_to_all | solution.py:237
  458.7 15.6 %all-to-all-done.3 = bf16[8,64,1024]{2,1,0:T(8,128)(2,1)S(1)} async-done(((bf16[8,64,1024]{2,1,0:T(8,128)(2,1)}), bf16[8,64,1024]{2,1,0:T(8,128)(2,1)S(1)}, u32[]{:S(2)}, u32[]{:S(2)}) %all-to-all-start.3) | async-done | bytes 1048608 | tf_op jit(solution)/shard_map/all_to_all | solution.py:234
  475.3 18.9 %fusion.56 = f32[256,8192]{1,0:T(8,128)} fusion(bf16[256,1024]{1,0:T(8,128)(2,1)S(1)} %bitcast.128, bf16[8192,1024]{1,0:T(8,128)(2,1)} %param.16), kind=kOutput, calls=%fused_computation.91 | convolution fusion | flops 4294967296 | bytes 25690112 | tf_op jit(solution)/shard_map/dot_general | solution.py:43
  494.2 6.1 %convolution_add_fusion.1 = f32[256,8192]{1,0:T(8,128)S(1)} fusion(f32[256,8192]{1,0:T(8,128)} %fusion.56, bf16[256,256]{1,0:T(8,128)(2,1)S(1)} %bitcast.133, bf16[8192,256]{1,0:T(8,128)(2,1)} %param.17), kind=kOutput, calls=%fused_computation.39 | convolution fusion | flops 1075838976 | bytes 21102592 | tf_op jit(solution)/shard_map/dot_general | solution.py:43
  506.2 40.6 %reduce-scatter.2.cloned.1.call-done = bf16[256,2048]{1,0:T(8,128)(2,1)} async-done(((bf16[256,8192]{1,0:T(8,128)(2,1)}), bf16[256,2048]{1,0:T(8,128)(2,1)}) %reduce-scatter.2.cloned.1.call-update) | async-done | bytes 1048592 | tf_op jit(solution)/shard_map/reduce_scatter | solution.py:259
  (367 shorter events, 319.0 us)
Async XLA Ops:
  7.2 39.6 %all-gather.4.cloned.1.call-start = ((), (), s32[]{:S(2)}) async-start(), calls=%async_computation.7 | async-start | bytes 5242880 | tf_op jit(solution)/shard_map/all_gather | solution.py:62
  67.4 18.4 %all-to-all-start = ((bf16[8,64,256]{2,1,0:T(8,128)(2,1)}), bf16[8,64,256]{2,1,0:T(8,128)(2,1)S(1)}, u32[]{:S(2)}, u32[]{:S(2)}) async-start(bf16[8,64,256]{2,1,0:T(8,128)(2,1)} %copy.103), calls=%async_computation | async-start | bytes 524288 | tf_op jit(solution)/shard_map/all_to_all | solution.py:80
  71.0 57.1 %all-gather.8.cloned.1.call-start = ((), (), s32[]{:S(2)}) async-start(), calls=%async_computation.9 | async-start | bytes 1179648 | tf_op jit(solution)/shard_map/all_gather | solution.py:189
  85.8 39.7 %all-to-all-start.1 = ((bf16[8,64,1024]{2,1,0:T(8,128)(2,1)}), bf16[8,64,1024]{2,1,0:T(8,128)(2,1)S(1)}, u32[]{:S(2)}, u32[]{:S(2)}) async-start(bf16[8,64,1024]{2,1,0:T(8,128)(2,1)} %copy.107), calls=%async_computation.1 | async-start | bytes 2097152 | tf_op jit(solution)/shard_map/all_to_all | solution.py:77
  91.8 74.8 %all-gather.6.cloned.1.call-start = ((), (), s32[]{:S(2)}) async-start(), calls=%async_computation.8 | async-start | bytes 1179648 | tf_op jit(solution)/shard_map/all_gather | solution.py:188
  224.0 23.6 %collective-permute-start = (bf16[256,256]{1,0:T(8,128)(2,1)}, bf16[256,256]{1,0:T(8,128)(2,1)}, u32[]{:S(2)}, u32[]{:S(2)}) collective-permute-start(bf16[256,256]{1,0:T(8,128)(2,1)} %copy.227), channel_id=1, source_target_pairs={{0,4},{4,8},{8,12},{12,16},{16,20},{20,24},{24,28},{28,0},{1,5},{5... | collective-permute-start | bytes 393224 | tf_op jit(solution)/shard_map/while/body/eval_jaxpr/ppermute | solution.py:15
  226.1 21.5 %collective-permute-start.1 = (bf16[256,256]{1,0:T(8,128)(2,1)}, bf16[256,256]{1,0:T(8,128)(2,1)}, u32[]{:S(2)}, u32[]{:S(2)}) collective-permute-start(bf16[256,256]{1,0:T(8,128)(2,1)} %copy.228), channel_id=1, source_target_pairs={{0,4},{4,8},{8,12},{12,16},{16,20},{20,24},{24,28},{28,0},{1,5},{5... | collective-permute-start | bytes 393224 | tf_op jit(solution)/shard_map/while/body/eval_jaxpr/ppermute | solution.py:15
  249.2 22.0 %collective-permute-start = (bf16[256,256]{1,0:T(8,128)(2,1)}, bf16[256,256]{1,0:T(8,128)(2,1)}, u32[]{:S(2)}, u32[]{:S(2)}) collective-permute-start(bf16[256,256]{1,0:T(8,128)(2,1)} %copy.227), channel_id=1, source_target_pairs={{0,4},{4,8},{8,12},{12,16},{16,20},{20,24},{24,28},{28,0},{1,5},{5... | collective-permute-start | bytes 393224 | tf_op jit(solution)/shard_map/while/body/eval_jaxpr/ppermute | solution.py:15
  250.8 20.4 %collective-permute-start.1 = (bf16[256,256]{1,0:T(8,128)(2,1)}, bf16[256,256]{1,0:T(8,128)(2,1)}, u32[]{:S(2)}, u32[]{:S(2)}) collective-permute-start(bf16[256,256]{1,0:T(8,128)(2,1)} %copy.228), channel_id=1, source_target_pairs={{0,4},{4,8},{8,12},{12,16},{16,20},{20,24},{24,28},{28,0},{1,5},{5... | collective-permute-start | bytes 393224 | tf_op jit(solution)/shard_map/while/body/eval_jaxpr/ppermute | solution.py:15
  272.8 23.7 %collective-permute-start = (bf16[256,256]{1,0:T(8,128)(2,1)}, bf16[256,256]{1,0:T(8,128)(2,1)}, u32[]{:S(2)}, u32[]{:S(2)}) collective-permute-start(bf16[256,256]{1,0:T(8,128)(2,1)} %copy.227), channel_id=1, source_target_pairs={{0,4},{4,8},{8,12},{12,16},{16,20},{20,24},{24,28},{28,0},{1,5},{5... | collective-permute-start | bytes 393224 | tf_op jit(solution)/shard_map/while/body/eval_jaxpr/ppermute | solution.py:15
  274.4 22.1 %collective-permute-start.1 = (bf16[256,256]{1,0:T(8,128)(2,1)}, bf16[256,256]{1,0:T(8,128)(2,1)}, u32[]{:S(2)}, u32[]{:S(2)}) collective-permute-start(bf16[256,256]{1,0:T(8,128)(2,1)} %copy.228), channel_id=1, source_target_pairs={{0,4},{4,8},{8,12},{12,16},{16,20},{20,24},{24,28},{28,0},{1,5},{5... | collective-permute-start | bytes 393224 | tf_op jit(solution)/shard_map/while/body/eval_jaxpr/ppermute | solution.py:15
  298.1 23.9 %collective-permute-start = (bf16[256,256]{1,0:T(8,128)(2,1)}, bf16[256,256]{1,0:T(8,128)(2,1)}, u32[]{:S(2)}, u32[]{:S(2)}) collective-permute-start(bf16[256,256]{1,0:T(8,128)(2,1)} %copy.227), channel_id=1, source_target_pairs={{0,4},{4,8},{8,12},{12,16},{16,20},{20,24},{24,28},{28,0},{1,5},{5... | collective-permute-start | bytes 393224 | tf_op jit(solution)/shard_map/while/body/eval_jaxpr/ppermute | solution.py:15
  299.6 22.3 %collective-permute-start.1 = (bf16[256,256]{1,0:T(8,128)(2,1)}, bf16[256,256]{1,0:T(8,128)(2,1)}, u32[]{:S(2)}, u32[]{:S(2)}) collective-permute-start(bf16[256,256]{1,0:T(8,128)(2,1)} %copy.228), channel_id=1, source_target_pairs={{0,4},{4,8},{8,12},{12,16},{16,20},{20,24},{24,28},{28,0},{1,5},{5... | collective-permute-start | bytes 393224 | tf_op jit(solution)/shard_map/while/body/eval_jaxpr/ppermute | solution.py:15
  323.5 26.3 %collective-permute-start = (bf16[256,256]{1,0:T(8,128)(2,1)}, bf16[256,256]{1,0:T(8,128)(2,1)}, u32[]{:S(2)}, u32[]{:S(2)}) collective-permute-start(bf16[256,256]{1,0:T(8,128)(2,1)} %copy.227), channel_id=1, source_target_pairs={{0,4},{4,8},{8,12},{12,16},{16,20},{20,24},{24,28},{28,0},{1,5},{5... | collective-permute-start | bytes 393224 | tf_op jit(solution)/shard_map/while/body/eval_jaxpr/ppermute | solution.py:15
  325.1 24.7 %collective-permute-start.1 = (bf16[256,256]{1,0:T(8,128)(2,1)}, bf16[256,256]{1,0:T(8,128)(2,1)}, u32[]{:S(2)}, u32[]{:S(2)}) collective-permute-start(bf16[256,256]{1,0:T(8,128)(2,1)} %copy.228), channel_id=1, source_target_pairs={{0,4},{4,8},{8,12},{12,16},{16,20},{20,24},{24,28},{28,0},{1,5},{5... | collective-permute-start | bytes 393224 | tf_op jit(solution)/shard_map/while/body/eval_jaxpr/ppermute | solution.py:15
  351.3 21.6 %collective-permute-start = (bf16[256,256]{1,0:T(8,128)(2,1)}, bf16[256,256]{1,0:T(8,128)(2,1)}, u32[]{:S(2)}, u32[]{:S(2)}) collective-permute-start(bf16[256,256]{1,0:T(8,128)(2,1)} %copy.227), channel_id=1, source_target_pairs={{0,4},{4,8},{8,12},{12,16},{16,20},{20,24},{24,28},{28,0},{1,5},{5... | collective-permute-start | bytes 393224 | tf_op jit(solution)/shard_map/while/body/eval_jaxpr/ppermute | solution.py:15
  352.9 20.1 %collective-permute-start.1 = (bf16[256,256]{1,0:T(8,128)(2,1)}, bf16[256,256]{1,0:T(8,128)(2,1)}, u32[]{:S(2)}, u32[]{:S(2)}) collective-permute-start(bf16[256,256]{1,0:T(8,128)(2,1)} %copy.228), channel_id=1, source_target_pairs={{0,4},{4,8},{8,12},{12,16},{16,20},{20,24},{24,28},{28,0},{1,5},{5... | collective-permute-start | bytes 393224 | tf_op jit(solution)/shard_map/while/body/eval_jaxpr/ppermute | solution.py:15
  374.5 24.0 %collective-permute-start = (bf16[256,256]{1,0:T(8,128)(2,1)}, bf16[256,256]{1,0:T(8,128)(2,1)}, u32[]{:S(2)}, u32[]{:S(2)}) collective-permute-start(bf16[256,256]{1,0:T(8,128)(2,1)} %copy.227), channel_id=1, source_target_pairs={{0,4},{4,8},{8,12},{12,16},{16,20},{20,24},{24,28},{28,0},{1,5},{5... | collective-permute-start | bytes 393224 | tf_op jit(solution)/shard_map/while/body/eval_jaxpr/ppermute | solution.py:15
  376.1 22.5 %collective-permute-start.1 = (bf16[256,256]{1,0:T(8,128)(2,1)}, bf16[256,256]{1,0:T(8,128)(2,1)}, u32[]{:S(2)}, u32[]{:S(2)}) collective-permute-start(bf16[256,256]{1,0:T(8,128)(2,1)} %copy.228), channel_id=1, source_target_pairs={{0,4},{4,8},{8,12},{12,16},{16,20},{20,24},{24,28},{28,0},{1,5},{5... | collective-permute-start | bytes 393224 | tf_op jit(solution)/shard_map/while/body/eval_jaxpr/ppermute | solution.py:15
  400.1 25.2 %collective-permute-start = (bf16[256,256]{1,0:T(8,128)(2,1)}, bf16[256,256]{1,0:T(8,128)(2,1)}, u32[]{:S(2)}, u32[]{:S(2)}) collective-permute-start(bf16[256,256]{1,0:T(8,128)(2,1)} %copy.227), channel_id=1, source_target_pairs={{0,4},{4,8},{8,12},{12,16},{16,20},{20,24},{24,28},{28,0},{1,5},{5... | collective-permute-start | bytes 393224 | tf_op jit(solution)/shard_map/while/body/eval_jaxpr/ppermute | solution.py:15
  401.7 23.6 %collective-permute-start.1 = (bf16[256,256]{1,0:T(8,128)(2,1)}, bf16[256,256]{1,0:T(8,128)(2,1)}, u32[]{:S(2)}, u32[]{:S(2)}) collective-permute-start(bf16[256,256]{1,0:T(8,128)(2,1)} %copy.228), channel_id=1, source_target_pairs={{0,4},{4,8},{8,12},{12,16},{16,20},{20,24},{24,28},{28,0},{1,5},{5... | collective-permute-start | bytes 393224 | tf_op jit(solution)/shard_map/while/body/eval_jaxpr/ppermute | solution.py:15
  438.1 16.4 %all-to-all-start.4 = ((bf16[8,64,256]{2,1,0:T(8,128)(2,1)}), bf16[8,64,256]{2,1,0:T(8,128)(2,1)S(1)}, u32[]{:S(2)}, u32[]{:S(2)}) async-start(bf16[8,64,256]{2,1,0:T(8,128)(2,1)} %copy.127), calls=%async_computation.4 | async-start | bytes 524288 | tf_op jit(solution)/shard_map/all_to_all | solution.py:237
  454.5 19.9 %all-to-all-start.3 = ((bf16[8,64,1024]{2,1,0:T(8,128)(2,1)}), bf16[8,64,1024]{2,1,0:T(8,128)(2,1)S(1)}, u32[]{:S(2)}, u32[]{:S(2)}) async-start(bf16[8,64,1024]{2,1,0:T(8,128)(2,1)} %copy.122), calls=%async_computation.3 | async-start | bytes 2097152 | tf_op jit(solution)/shard_map/all_to_all | solution.py:234
  458.0 88.7 %reduce-scatter.2.cloned.1.call-start = ((), (), s32[]{:S(2)}) async-start(), calls=%async_computation.10 | async-start | bytes 5242880 | tf_op jit(solution)/shard_map/reduce_scatter | solution.py:259
  (42 other events, 635.8 us)
Sparse Core Ops, SparseCore 0:
  9.6 37.1 all-gather.3
  74.0 51.0 all-gather.7
  127.2 39.3 all-gather.5
  503.7 43.0 reduce-scatter.1
where the time goes:
time: 556 us; the launch traced here: 553 us
  waiting for transfers between devices  231 us (42%)
  matrix products  104 us (19%)
  local copies, waits for them, and re-layouts  90.9 us (16%)
  starting transfers between devices  56.4 us (10%)
  other arithmetic  49 us (9%)
  between operations  14.1 us (3%)
  loops' own time  8.15 us (1%)
    ppermute x32, waiting for transfers between devices, from_behind(): return lax.ppermute(value, axis, pairs)  53.3 us
    reduce_scatter x1, waiting for transfers between devices, per_device(): lax.psum_scatter(grad_terms.astype(jnp.bfloat16), 'heads', scatter_dimens...  40.6 us
    all_gather x1, waiting for transfers between devices, per_device(): piece = lax.all_gather(activations, 'heads', axis=1, tiled=True)  37.1 us
    all_gather x1, waiting for transfers between devices, per_device(): key_piece = lax.all_gather(ctx_k, 'ctx', axis=0, tiled=True)  36.9 us
    ppermute x32, starting transfers between devices, from_behind(): return lax.ppermute(value, axis, pairs)  30.5 us
    dot_general x3, matrix products, transposed_dot(): lax.dot_general(left, weight, (((1,), (1,)), ((), ())), preferred_element...  28.3 us
    all_to_all x1, waiting for transfers between devices, per_device(): lax.all_to_all(spread(send_map, loader_q, block_rows), 'ctx', split_axis=...  27.5 us
    while x16, local copies, waits for them, and re-layouts  25 us
  transfers between devices with their start and end apart: 42, of which 24 were waited for; matrix products, arithmetic and copies ran while one was open for 25% of the time, Pallas kernels for 0%

commit v1 on v0

--- a/solution.py
+++ b/solution.py
@@ -185,7 +185,12 @@
         return lax.fori_loop(0, rows // width, grads_one_block, (dquery, empty_rows, empty_rows))
 
     dq_start = jnp.zeros((tok_dev, groups, per_group, head_dim), jnp.float32)
-    key_piece = lax.all_gather(ctx_k, "ctx", axis=0, tiled=True)
+    ring = [ctx_k]
+    for hop in range(7):
+        ring.append(lax.ppermute(ring[-1], "ctx", [(dev, (dev + 1) % 8) for dev in range(8)]))
+    key_piece = jnp.roll(
+        jnp.concatenate(ring[::-1], axis=0), (lax.axis_index("ctx") + 1) * ring[0].shape[0], axis=0
+    )
     value_piece = lax.all_gather(ctx_v, "ctx", axis=0, tiled=True)
     rows = key_piece.shape[0]
     width = math.gcd(rows, 512)

time: 556 us -> 562 us (1.011)
  waiting for transfers between devices: 231 us -> 222 us
  local copies, waits for them, and re-layouts: 90.9 us -> 97.3 us
  starting transfers between devices: 56.4 us -> 62.2 us
    all_gather x1 -> x0, waiting for transfers between devices: 36.9 us -> none  [per_device(): key_piece = lax.all_gather(ctx_k, 'ctx', axis=0, tiled=True)]
    ppermute x0 -> x7, waiting for transfers between devices: none -> 20 us  [per_device(): lax.ppermute(ring[-1], 'ctx', [(dev, (dev + 1) % 8) for dev in range(8)])]
    all_gather x1, waiting for transfers between devices: 0.02 us -> 16.3 us  [per_device(): value_piece = lax.all_gather(ctx_v, 'ctx', axis=0, tiled=True)]
    all_to_all x1, waiting for transfers between devices: 27.5 us -> 12.6 us  [per_device(): lax.all_to_all(spread(send_map, loader_q, block_rows), 'ctx', split_axis=...]
    all_to_all x1, waiting for transfers between devices: 0.01 us -> 8.93 us  [per_device(): lax.all_to_all(spread(send_map, loader_k, block_rows), 'ctx', split_axis=...]
  transfers between devices with their start and end apart: 42 -> 48, of which waited for: 24 -> 30; matrix products, arithmetic and copies ran while one was open for 25% -> 26% of each run, Pallas kernels for 0% -> 0%
where the time goes in v1:
time: 562 us; the launch traced here: 559 us
  waiting for transfers between devices  222 us (40%)
  matrix products  105 us (19%)
  local copies, waits for them, and re-layouts  97.3 us (17%)
  starting transfers between devices  62.2 us (11%)
  other arithmetic  48.4 us (9%)
  between operations  14.2 us (3%)
  loops' own time  9.13 us (2%)
    ppermute x32, waiting for transfers between devices, from_behind(): return lax.ppermute(value, axis, pairs)  53.5 us
    reduce_scatter x1, waiting for transfers between devices, per_device(): lax.psum_scatter(grad_terms.astype(jnp.bfloat16), 'heads', scatter_dimens...  40.4 us
    all_gather x1, waiting for transfers between devices, per_device(): piece = lax.all_gather(activations, 'heads', axis=1, tiled=True)  38.1 us
    ppermute x32, starting transfers between devices, from_behind(): return lax.ppermute(value, axis, pairs)  30.4 us
    dot_general x3, matrix products, transposed_dot(): lax.dot_general(left, weight, (((1,), (1,)), ((), ())), preferred_element...  28.6 us
    while x16, local copies, waits for them, and re-layouts  25.2 us
    ppermute x7, waiting for transfers between devices, per_device(): lax.ppermute(ring[-1], 'ctx', [(dev, (dev + 1) % 8) for dev in range(8)])  20 us
    dot_general x4, matrix products, attend_run(): jnp.einsum('gqts,sge->gqte', probs, value_blk.astype(jnp.float32), precis...  16.8 us
  transfers between devices with their start and end apart: 48, of which 30 were waited for; matrix products, arithmetic and copies ran while one was open for 26% of the time, Pallas kernels for 0%

profile of v1, /device:TPU:0, one launch (start us, length us, event | category | flops | bytes accessed | tf_op | source)
XLA Modules:
  0.0 559.0 jit_solution(11764167370304066795)
XLA Ops:
  8.6 38.1 %all-gather.3.cloned.1.call-done = bf16[256,8192]{1,0:T(8,128)(2,1)} async-done(((bf16[256,2048]{1,0:T(8,128)(2,1)}), bf16[256,8192]{1,0:T(8,128)(2,1)}) %all-gather.3.cloned.1.call-update) | async-done | bytes 4194320 | tf_op jit(solution)/shard_map/all_gather | solution.py:62
  58.5 8.9 %all-to-all-done = bf16[8,64,256]{2,1,0:T(8,128)(2,1)S(1)} async-done(((bf16[8,64,256]{2,1,0:T(8,128)(2,1)}), bf16[8,64,256]{2,1,0:T(8,128)(2,1)S(1)}, u32[]{:S(2)}, u32[]{:S(2)}) %all-to-all-start) | async-done | bytes 262176 | tf_op jit(solution)/shard_map/all_to_all | solution.py:80
  69.8 6.5 %collective-permute-done.4 = bf16[256,256]{1,0:T(8,128)(2,1)S(1)} collective-permute-done((bf16[256,256]{1,0:T(8,128)(2,1)}, bf16[256,256]{1,0:T(8,128)(2,1)S(1)}, u32[]{:S(2)}, u32[]{:S(2)}) %collective-permute-start.4) | collective-permute-done | bytes 131104 | tf_op jit(solution)/shard_map/ppermute | solution.py:190
  92.7 6.0 %all-to-all-start.2 = ((bf16[8,64,256]{2,1,0:T(8,128)(2,1)}), bf16[8,64,256]{2,1,0:T(8,128)(2,1)S(1)}, u32[]{:S(2)}, u32[]{:S(2)}) async-start(bf16[8,64,256]{2,1,0:T(8,128)(2,1)} %copy.111), calls=%async_computation.2 | async-start | bytes 524288 | tf_op jit(solution)/shard_map/all_to_all | solution.py:83
  100.7 11.5 %convolution_convert_fusion.4 = bf16[256,1024]{1,0:T(8,128)(2,1)S(1)} fusion(bf16[256,8192]{1,0:T(8,128)(2,1)} %all-gather.3.cloned.1.call-done, bf16[8192,1024]{1,0:T(8,128)(2,1)} %param.16), kind=kOutput, calls=%fused_computation.45 | convolution fusion | flops 4295229440 | bytes 21495808 | tf_op jit(solution)/shard_map/dot_general | solution.py:64
  120.9 6.0 %all-to-all-start.1 = ((bf16[8,64,1024]{2,1,0:T(8,128)(2,1)}), bf16[8,64,1024]{2,1,0:T(8,128)(2,1)}, u32[]{:S(2)}, u32[]{:S(2)}) async-start(bf16[8,64,1024]{2,1,0:T(8,128)(2,1)} %copy.107), calls=%async_computation.1 | async-start | bytes 2097152 | tf_op jit(solution)/shard_map/all_to_all | solution.py:77
  134.7 12.6 %all-to-all-done.1 = bf16[8,64,1024]{2,1,0:T(8,128)(2,1)} async-done(((bf16[8,64,1024]{2,1,0:T(8,128)(2,1)}), bf16[8,64,1024]{2,1,0:T(8,128)(2,1)}, u32[]{:S(2)}, u32[]{:S(2)}) %all-to-all-start.1) | async-done | bytes 1048608 | tf_op jit(solution)/shard_map/all_to_all | solution.py:77
  154.7 16.3 %all-gather.5.cloned.1.call-done = bf16[2048,256]{1,0:T(8,128)(2,1)} async-done(((bf16[256,256]{1,0:T(8,128)(2,1)}), bf16[2048,256]{1,0:T(8,128)(2,1)}) %all-gather.5.cloned.1.call-update) | async-done | bytes 1048592 | tf_op jit(solution)/shard_map/all_gather | solution.py:194
  174.4 47.7 %while.56 = (s32[]{:T(128)}, f32[2,4,256]{2,1,0:T(4,128)S(1)}, f32[2,4,256]{2,1,0:T(4,128)S(1)}, f32[2,4,256,128]{3,2,1,0:T(8,128)}, s32[256]{0:T(256)}, /*index...) while((s32[]{:T(128)}, f32[2,4,256]{2,1,0:T(4,128)S(1)}, ...), condition=%wide.region_10.11_spmd, body=%wide.region_4.10_spmd.sunk | while | flops 1892683776 | bytes 25835900 | solution.py:210
  178.1 8.2 %conditional.5 = ((f32[2,4,256]{2,1,0:T(4,128)S(1)}, f32[2,4,256]{2,1,0:T(4,128)S(1)}, f32[2,4,256,128]{3,2,1,0:T(8,128)})) conditional(s32[]{:T(128)} %convert_element_type.201, (f32[2,4,256]{2,1,0:T(4,128)S(1)}, f32[2,4,256]{2,1,0:T(4,128)S(1)}, f32[2,4,256,128]{3,2,1,0:T(8,128)}) %tuple.116, (pred[256,512]{0,1:T(8,128)(4,1)S(1)}, ...), branch_computations={%region_6.6_spmd, %region_7.9_spmd} | conditional | flops 1892159488 | bytes 25690204 | solution.py:126
  190.0 8.2 %conditional.5 = ((f32[2,4,256]{2,1,0:T(4,128)S(1)}, f32[2,4,256]{2,1,0:T(4,128)S(1)}, f32[2,4,256,128]{3,2,1,0:T(8,128)})) conditional(s32[]{:T(128)} %convert_element_type.201, (f32[2,4,256]{2,1,0:T(4,128)S(1)}, f32[2,4,256]{2,1,0:T(4,128)S(1)}, f32[2,4,256,128]{3,2,1,0:T(8,128)}) %tuple.116, (pred[256,512]{0,1:T(8,128)(4,1)S(1)}, ...), branch_computations={%region_6.6_spmd, %region_7.9_spmd} | conditional | flops 1892159488 | bytes 25690204 | solution.py:126
  201.9 8.2 %conditional.5 = ((f32[2,4,256]{2,1,0:T(4,128)S(1)}, f32[2,4,256]{2,1,0:T(4,128)S(1)}, f32[2,4,256,128]{3,2,1,0:T(8,128)})) conditional(s32[]{:T(128)} %convert_element_type.201, (f32[2,4,256]{2,1,0:T(4,128)S(1)}, f32[2,4,256]{2,1,0:T(4,128)S(1)}, f32[2,4,256,128]{3,2,1,0:T(8,128)}) %tuple.116, (pred[256,512]{0,1:T(8,128)(4,1)S(1)}, ...), branch_computations={%region_6.6_spmd, %region_7.9_spmd} | conditional | flops 1892159488 | bytes 25690204 | solution.py:126
  213.9 8.2 %conditional.5 = ((f32[2,4,256]{2,1,0:T(4,128)S(1)}, f32[2,4,256]{2,1,0:T(4,128)S(1)}, f32[2,4,256,128]{3,2,1,0:T(8,128)})) conditional(s32[]{:T(128)} %convert_element_type.201, (f32[2,4,256]{2,1,0:T(4,128)S(1)}, f32[2,4,256]{2,1,0:T(4,128)S(1)}, f32[2,4,256,128]{3,2,1,0:T(8,128)}) %tuple.116, (pred[256,512]{0,1:T(8,128)(4,1)S(1)}, ...), branch_computations={%region_6.6_spmd, %region_7.9_spmd} | conditional | flops 1892159488 | bytes 25690204 | solution.py:126
  227.0 203.8 %while.57 = (s32[]{:T(128)}, f32[256,2,4,128]{3,0,2,1:T(8,128)S(1)}, bf16[256,256]{1,0:T(8,128)(2,1)}, bf16[256,256]{1,0:T(8,128)(2,1)}, f32[256,256]{0,1:T(8,12...) while((s32[]{:T(128)}, ...), condition=%wide.region_15.16_spmd.clone, body=%wide.region_11.15_spmd.clone.sunk | while | flops 676593664 | bytes 24142468 | solution.py:231
  309.1 5.6 %conditional.6 = (f32[256,2,4,128]{3,0,2,1:T(8,128)S(1)}, f32[256,256]{0,1:T(8,128)S(1)}, f32[256,256]{0,1:T(8,128)S(1)}) conditional(s32[]{:T(128)} %convert_element_type.204, () %tuple.120, (pred[256,256]{0,1:T(8,128)(4,1)}, bf16[256,256]{1,0:T(8,128)(2,1)}, bf16[256,2,4,128]{0,3,2,1:T(8,128)(2,1)}, f32[2,4,256]{2,1,0:T(4,128)}, ...), branch_computations={%region_13.13_spmd, %region_14.14_spmd} | conditional | flops 675282944 | bytes 16203828 | solution.py:179
  344.5 6.9 %collective-permute-done.3 = bf16[256,256]{0,1:T(8,128)(2,1)S(1)} collective-permute-done((bf16[256,256]{0,1:T(8,128)(2,1)S(1)}, bf16[256,256]{0,1:T(8,128)(2,1)S(1)}, u32[]{:S(2)}, u32[]{:S(2)}) %collective-permute-start.3) | collective-permute-done | bytes 131104 | tf_op jit(solution)/shard_map/while/body/eval_jaxpr/ppermute | solution.py:15
  386.8 5.6 conditional.6
  422.0 6.1 %collective-permute-done.3 = bf16[256,256]{0,1:T(8,128)(2,1)S(1)} collective-permute-done((bf16[256,256]{0,1:T(8,128)(2,1)S(1)}, bf16[256,256]{0,1:T(8,128)(2,1)S(1)}, u32[]{:S(2)}, u32[]{:S(2)}) %collective-permute-start.3) | collective-permute-done | bytes 131104 | tf_op jit(solution)/shard_map/while/body/eval_jaxpr/ppermute | solution.py:15
  437.6 6.0 %all-to-all-done.5 = bf16[8,64,256]{2,1,0:T(8,128)(2,1)S(1)} async-done(((bf16[8,64,256]{2,1,0:T(8,128)(2,1)}), bf16[8,64,256]{2,1,0:T(8,128)(2,1)S(1)}, u32[]{:S(2)}, u32[]{:S(2)}) %all-to-all-start.5) | async-done | bytes 262176 | tf_op jit(solution)/shard_map/all_to_all | solution.py:245
  450.1 10.0 %all-to-all-done.4 = bf16[8,64,256]{2,1,0:T(8,128)(2,1)S(1)} async-done(((bf16[8,64,256]{2,1,0:T(8,128)(2,1)}), bf16[8,64,256]{2,1,0:T(8,128)(2,1)S(1)}, u32[]{:S(2)}, u32[]{:S(2)}) %all-to-all-start.4) | async-done | bytes 262176 | tf_op jit(solution)/shard_map/all_to_all | solution.py:242
  464.3 15.6 %all-to-all-done.3 = bf16[8,64,1024]{2,1,0:T(8,128)(2,1)S(1)} async-done(((bf16[8,64,1024]{2,1,0:T(8,128)(2,1)}), bf16[8,64,1024]{2,1,0:T(8,128)(2,1)S(1)}, u32[]{:S(2)}, u32[]{:S(2)}) %all-to-all-start.3) | async-done | bytes 1048608 | tf_op jit(solution)/shard_map/all_to_all | solution.py:239
  480.9 19.2 %fusion.56 = f32[256,8192]{1,0:T(8,128)} fusion(bf16[256,1024]{1,0:T(8,128)(2,1)S(1)} %bitcast.128, bf16[8192,1024]{1,0:T(8,128)(2,1)} %param.16), kind=kOutput, calls=%fused_computation.108 | convolution fusion | flops 4294967296 | bytes 25690112 | tf_op jit(solution)/shard_map/dot_general | solution.py:43
  500.1 6.1 %convolution_add_fusion.1 = f32[256,8192]{1,0:T(8,128)S(1)} fusion(f32[256,8192]{1,0:T(8,128)} %fusion.56, bf16[256,256]{1,0:T(8,128)(2,1)S(1)} %bitcast.133, bf16[8192,256]{1,0:T(8,128)(2,1)} %param.17), kind=kOutput, calls=%fused_computation.39 | convolution fusion | flops 1075838976 | bytes 21102592 | tf_op jit(solution)/shard_map/dot_general | solution.py:43
  512.1 40.4 %reduce-scatter.2.cloned.1.call-done = bf16[256,2048]{1,0:T(8,128)(2,1)} async-done(((bf16[256,8192]{1,0:T(8,128)(2,1)}), bf16[256,2048]{1,0:T(8,128)(2,1)}) %reduce-scatter.2.cloned.1.call-update) | async-done | bytes 1048592 | tf_op jit(solution)/shard_map/reduce_scatter | solution.py:264
  (399 shorter events, 352.9 us)
Async XLA Ops:
  7.2 39.6 %all-gather.3.cloned.1.call-start = ((), (), s32[]{:S(2)}) async-start(), calls=%async_computation.7 | async-start | bytes 5242880 | tf_op jit(solution)/shard_map/all_gather | solution.py:62
  52.6 14.8 %all-to-all-start = ((bf16[8,64,256]{2,1,0:T(8,128)(2,1)}), bf16[8,64,256]{2,1,0:T(8,128)(2,1)S(1)}, u32[]{:S(2)}, u32[]{:S(2)}) async-start(bf16[8,64,256]{2,1,0:T(8,128)(2,1)} %copy.103), calls=%async_computation | async-start | bytes 524288 | tf_op jit(solution)/shard_map/all_to_all | solution.py:80
  92.7 28.2 %all-to-all-start.2 = ((bf16[8,64,256]{2,1,0:T(8,128)(2,1)}), bf16[8,64,256]{2,1,0:T(8,128)(2,1)S(1)}, u32[]{:S(2)}, u32[]{:S(2)}) async-start(bf16[8,64,256]{2,1,0:T(8,128)(2,1)} %copy.111), calls=%async_computation.2 | async-start | bytes 524288 | tf_op jit(solution)/shard_map/all_to_all | solution.py:83
  120.9 26.4 %all-to-all-start.1 = ((bf16[8,64,1024]{2,1,0:T(8,128)(2,1)}), bf16[8,64,1024]{2,1,0:T(8,128)(2,1)}, u32[]{:S(2)}, u32[]{:S(2)}) async-start(bf16[8,64,1024]{2,1,0:T(8,128)(2,1)} %copy.107), calls=%async_computation.1 | async-start | bytes 2097152 | tf_op jit(solution)/shard_map/all_to_all | solution.py:77
  126.9 44.2 %all-gather.5.cloned.1.call-start = ((), (), s32[]{:S(2)}) async-start(), calls=%async_computation.8 | async-start | bytes 1179648 | tf_op jit(solution)/shard_map/all_gather | solution.py:194
  228.8 23.7 %collective-permute-start = (bf16[256,256]{1,0:T(8,128)(2,1)}, bf16[256,256]{1,0:T(8,128)(2,1)}, u32[]{:S(2)}, u32[]{:S(2)}) collective-permute-start(bf16[256,256]{1,0:T(8,128)(2,1)} %copy.242), channel_id=1, source_target_pairs={{0,4},{4,8},{8,12},{12,16},{16,20},{20,24},{24,28},{28,0},{1,5},{5... | collective-permute-start | bytes 393224 | tf_op jit(solution)/shard_map/while/body/eval_jaxpr/ppermute | solution.py:15
  231.0 21.6 %collective-permute-start.1 = (bf16[256,256]{1,0:T(8,128)(2,1)}, bf16[256,256]{1,0:T(8,128)(2,1)}, u32[]{:S(2)}, u32[]{:S(2)}) collective-permute-start(bf16[256,256]{1,0:T(8,128)(2,1)} %copy.243), channel_id=1, source_target_pairs={{0,4},{4,8},{8,12},{12,16},{16,20},{20,24},{24,28},{28,0},{1,5},{5... | collective-permute-start | bytes 393224 | tf_op jit(solution)/shard_map/while/body/eval_jaxpr/ppermute | solution.py:15
  254.1 22.1 %collective-permute-start = (bf16[256,256]{1,0:T(8,128)(2,1)}, bf16[256,256]{1,0:T(8,128)(2,1)}, u32[]{:S(2)}, u32[]{:S(2)}) collective-permute-start(bf16[256,256]{1,0:T(8,128)(2,1)} %copy.242), channel_id=1, source_target_pairs={{0,4},{4,8},{8,12},{12,16},{16,20},{20,24},{24,28},{28,0},{1,5},{5... | collective-permute-start | bytes 393224 | tf_op jit(solution)/shard_map/while/body/eval_jaxpr/ppermute | solution.py:15
  255.7 20.5 %collective-permute-start.1 = (bf16[256,256]{1,0:T(8,128)(2,1)}, bf16[256,256]{1,0:T(8,128)(2,1)}, u32[]{:S(2)}, u32[]{:S(2)}) collective-permute-start(bf16[256,256]{1,0:T(8,128)(2,1)} %copy.243), channel_id=1, source_target_pairs={{0,4},{4,8},{8,12},{12,16},{16,20},{20,24},{24,28},{28,0},{1,5},{5... | collective-permute-start | bytes 393224 | tf_op jit(solution)/shard_map/while/body/eval_jaxpr/ppermute | solution.py:15
  277.8 23.8 %collective-permute-start = (bf16[256,256]{1,0:T(8,128)(2,1)}, bf16[256,256]{1,0:T(8,128)(2,1)}, u32[]{:S(2)}, u32[]{:S(2)}) collective-permute-start(bf16[256,256]{1,0:T(8,128)(2,1)} %copy.242), channel_id=1, source_target_pairs={{0,4},{4,8},{8,12},{12,16},{16,20},{20,24},{24,28},{28,0},{1,5},{5... | collective-permute-start | bytes 393224 | tf_op jit(solution)/shard_map/while/body/eval_jaxpr/ppermute | solution.py:15
  279.4 22.2 %collective-permute-start.1 = (bf16[256,256]{1,0:T(8,128)(2,1)}, bf16[256,256]{1,0:T(8,128)(2,1)}, u32[]{:S(2)}, u32[]{:S(2)}) collective-permute-start(bf16[256,256]{1,0:T(8,128)(2,1)} %copy.243), channel_id=1, source_target_pairs={{0,4},{4,8},{8,12},{12,16},{16,20},{20,24},{24,28},{28,0},{1,5},{5... | collective-permute-start | bytes 393224 | tf_op jit(solution)/shard_map/while/body/eval_jaxpr/ppermute | solution.py:15
  303.1 23.7 %collective-permute-start = (bf16[256,256]{1,0:T(8,128)(2,1)}, bf16[256,256]{1,0:T(8,128)(2,1)}, u32[]{:S(2)}, u32[]{:S(2)}) collective-permute-start(bf16[256,256]{1,0:T(8,128)(2,1)} %copy.242), channel_id=1, source_target_pairs={{0,4},{4,8},{8,12},{12,16},{16,20},{20,24},{24,28},{28,0},{1,5},{5... | collective-permute-start | bytes 393224 | tf_op jit(solution)/shard_map/while/body/eval_jaxpr/ppermute | solution.py:15
  304.7 22.1 %collective-permute-start.1 = (bf16[256,256]{1,0:T(8,128)(2,1)}, bf16[256,256]{1,0:T(8,128)(2,1)}, u32[]{:S(2)}, u32[]{:S(2)}) collective-permute-start(bf16[256,256]{1,0:T(8,128)(2,1)} %copy.243), channel_id=1, source_target_pairs={{0,4},{4,8},{8,12},{12,16},{16,20},{20,24},{24,28},{28,0},{1,5},{5... | collective-permute-start | bytes 393224 | tf_op jit(solution)/shard_map/while/body/eval_jaxpr/ppermute | solution.py:15
  328.4 26.2 %collective-permute-start = (bf16[256,256]{1,0:T(8,128)(2,1)}, bf16[256,256]{1,0:T(8,128)(2,1)}, u32[]{:S(2)}, u32[]{:S(2)}) collective-permute-start(bf16[256,256]{1,0:T(8,128)(2,1)} %copy.242), channel_id=1, source_target_pairs={{0,4},{4,8},{8,12},{12,16},{16,20},{20,24},{24,28},{28,0},{1,5},{5... | collective-permute-start | bytes 393224 | tf_op jit(solution)/shard_map/while/body/eval_jaxpr/ppermute | solution.py:15
  329.9 24.7 %collective-permute-start.1 = (bf16[256,256]{1,0:T(8,128)(2,1)}, bf16[256,256]{1,0:T(8,128)(2,1)}, u32[]{:S(2)}, u32[]{:S(2)}) collective-permute-start(bf16[256,256]{1,0:T(8,128)(2,1)} %copy.243), channel_id=1, source_target_pairs={{0,4},{4,8},{8,12},{12,16},{16,20},{20,24},{24,28},{28,0},{1,5},{5... | collective-permute-start | bytes 393224 | tf_op jit(solution)/shard_map/while/body/eval_jaxpr/ppermute | solution.py:15
  356.2 22.7 %collective-permute-start = (bf16[256,256]{1,0:T(8,128)(2,1)}, bf16[256,256]{1,0:T(8,128)(2,1)}, u32[]{:S(2)}, u32[]{:S(2)}) collective-permute-start(bf16[256,256]{1,0:T(8,128)(2,1)} %copy.242), channel_id=1, source_target_pairs={{0,4},{4,8},{8,12},{12,16},{16,20},{20,24},{24,28},{28,0},{1,5},{5... | collective-permute-start | bytes 393224 | tf_op jit(solution)/shard_map/while/body/eval_jaxpr/ppermute | solution.py:15
  357.7 21.1 %collective-permute-start.1 = (bf16[256,256]{1,0:T(8,128)(2,1)}, bf16[256,256]{1,0:T(8,128)(2,1)}, u32[]{:S(2)}, u32[]{:S(2)}) collective-permute-start(bf16[256,256]{1,0:T(8,128)(2,1)} %copy.243), channel_id=1, source_target_pairs={{0,4},{4,8},{8,12},{12,16},{16,20},{20,24},{24,28},{28,0},{1,5},{5... | collective-permute-start | bytes 393224 | tf_op jit(solution)/shard_map/while/body/eval_jaxpr/ppermute | solution.py:15
  380.4 23.0 %collective-permute-start = (bf16[256,256]{1,0:T(8,128)(2,1)}, bf16[256,256]{1,0:T(8,128)(2,1)}, u32[]{:S(2)}, u32[]{:S(2)}) collective-permute-start(bf16[256,256]{1,0:T(8,128)(2,1)} %copy.242), channel_id=1, source_target_pairs={{0,4},{4,8},{8,12},{12,16},{16,20},{20,24},{24,28},{28,0},{1,5},{5... | collective-permute-start | bytes 393224 | tf_op jit(solution)/shard_map/while/body/eval_jaxpr/ppermute | solution.py:15
  382.0 21.5 %collective-permute-start.1 = (bf16[256,256]{1,0:T(8,128)(2,1)}, bf16[256,256]{1,0:T(8,128)(2,1)}, u32[]{:S(2)}, u32[]{:S(2)}) collective-permute-start(bf16[256,256]{1,0:T(8,128)(2,1)} %copy.243), channel_id=1, source_target_pairs={{0,4},{4,8},{8,12},{12,16},{16,20},{20,24},{24,28},{28,0},{1,5},{5... | collective-permute-start | bytes 393224 | tf_op jit(solution)/shard_map/while/body/eval_jaxpr/ppermute | solution.py:15
  405.0 25.8 %collective-permute-start = (bf16[256,256]{1,0:T(8,128)(2,1)}, bf16[256,256]{1,0:T(8,128)(2,1)}, u32[]{:S(2)}, u32[]{:S(2)}) collective-permute-start(bf16[256,256]{1,0:T(8,128)(2,1)} %copy.242), channel_id=1, source_target_pairs={{0,4},{4,8},{8,12},{12,16},{16,20},{20,24},{24,28},{28,0},{1,5},{5... | collective-permute-start | bytes 393224 | tf_op jit(solution)/shard_map/while/body/eval_jaxpr/ppermute | solution.py:15
  406.6 24.2 %collective-permute-start.1 = (bf16[256,256]{1,0:T(8,128)(2,1)}, bf16[256,256]{1,0:T(8,128)(2,1)}, u32[]{:S(2)}, u32[]{:S(2)}) collective-permute-start(bf16[256,256]{1,0:T(8,128)(2,1)} %copy.243), channel_id=1, source_target_pairs={{0,4},{4,8},{8,12},{12,16},{16,20},{20,24},{24,28},{28,0},{1,5},{5... | collective-permute-start | bytes 393224 | tf_op jit(solution)/shard_map/while/body/eval_jaxpr/ppermute | solution.py:15
  443.6 16.5 %all-to-all-start.4 = ((bf16[8,64,256]{2,1,0:T(8,128)(2,1)}), bf16[8,64,256]{2,1,0:T(8,128)(2,1)S(1)}, u32[]{:S(2)}, u32[]{:S(2)}) async-start(bf16[8,64,256]{2,1,0:T(8,128)(2,1)} %copy.127), calls=%async_computation.4 | async-start | bytes 524288 | tf_op jit(solution)/shard_map/all_to_all | solution.py:242
  460.1 19.9 %all-to-all-start.3 = ((bf16[8,64,1024]{2,1,0:T(8,128)(2,1)}), bf16[8,64,1024]{2,1,0:T(8,128)(2,1)S(1)}, u32[]{:S(2)}, u32[]{:S(2)}) async-start(bf16[8,64,1024]{2,1,0:T(8,128)(2,1)} %copy.122), calls=%async_computation.3 | async-start | bytes 2097152 | tf_op jit(solution)/shard_map/all_to_all | solution.py:239
  463.6 88.9 %reduce-scatter.2.cloned.1.call-start = ((), (), s32[]{:S(2)}) async-start(), calls=%async_computation.9 | async-start | bytes 5242880 | tf_op jit(solution)/shard_map/reduce_scatter | solution.py:264
  (50 other events, 854.5 us)
Sparse Core Ops, SparseCore 0:
  9.6 37.1 all-gather.2
  129.8 41.1 all-gather.4
  509.6 42.8 reduce-scatter.1
